TPU v7x, 32 devices: a whole 2x2x4 slice. The times are simulated.
32 devices in a mesh: dp: 8 (over y, x, core), rep: 4 (over z).
Axes of the slice: x: 2, y: 2, z: 4, core: 2. Of those that a mesh axis runs over, the one named last changes fastest.
Arguments:
- audio_patches: bfloat16 [2, 64, 228, 256], P(None, ('dp', 'rep')), may hold values from -6 to 6
- clip_lengths: int32 [2, 64], P(None, ('dp', 'rep')), may hold values from 114 to 228, as said below
- video_ids: int32 [2, 64], P(None, ('dp', 'rep')), may hold values from 0 to 31
- image_tokens: bfloat16 [2, 64, 256, 1280], P(None, ('dp', 'rep')), may hold values from -6 to 6
- i_qkv: bfloat16 [1280, 3840], P('dp'), may hold values from -0.15625 to 0.15625
- i_out: bfloat16 [1280, 1280], P('dp'), may hold values from -0.625 to 0.625
- i_up: bfloat16 [1280, 5120], P('dp'), may hold values from -0.15625 to 0.15625
- i_down: bfloat16 [5120, 1280], P('dp'), may hold values from -0.078125 to 0.078125
- i_proj: bfloat16 [1280, 1024], P('dp'), may hold values from -0.15625 to 0.15625
- i_gains: bfloat16 [3, 1280], P(None, 'dp'), may hold values from 0.5 to 1.5
- a_patch: float32 [256, 768], P('dp'), may hold values from -0.375 to 0.375
- a_qkv: float32 [768, 2304], P('dp'), may hold values from -0.21875 to 0.21875
- a_out: float32 [768, 768], P('dp'), may hold values from -0.875 to 0.875
- a_up: float32 [768, 3072], P('dp'), may hold values from -0.21875 to 0.21875
- a_down: float32 [3072, 768], P('dp'), may hold values from -0.109375 to 0.109375
- a_proj: float32 [768, 1024], P('dp'), may hold values from -0.21875 to 0.21875
- a_gains: float32 [3, 768], P(None, 'dp'), may hold values from 0.5 to 1.5
- m_patch: float32 [256, 768], P('dp'), may hold values from -5.722046e-06 to 5.722046e-06
- m_qkv: float32 [768, 2304], P('dp'), may hold values from -5.722046e-06 to 5.722046e-06
- m_out: float32 [768, 768], P('dp'), may hold values from -5.722046e-06 to 5.722046e-06
- m_up: float32 [768, 3072], P('dp'), may hold values from -5.722046e-06 to 5.722046e-06
- m_down: float32 [3072, 768], P('dp'), may hold values from -5.722046e-06 to 5.722046e-06
- m_proj: float32 [768, 1024], P('dp'), may hold values from -5.722046e-06 to 5.722046e-06
- m_gains: float32 [3, 768], P(None, 'dp'), may hold values from -2.2888184e-05 to 2.2888184e-05
- s_patch: float32 [256, 768], P('dp'), may hold values from 1.2405519e-14 to 4.9622077e-14
- s_qkv: float32 [768, 2304], P('dp'), may hold values from 1.2405519e-14 to 4.9622077e-14
- s_out: float32 [768, 768], P('dp'), may hold values from 1.2405519e-14 to 4.9622077e-14
- s_up: float32 [768, 3072], P('dp'), may hold values from 1.2405519e-14 to 4.9622077e-14
- s_down: float32 [3072, 768], P('dp'), may hold values from 1.2405519e-14 to 4.9622077e-14
- s_proj: float32 [768, 1024], P('dp'), may hold values from 1.2405519e-14 to 4.9622077e-14
- s_gains: float32 [3, 768], P(None, 'dp'), may hold values from 1.9848831e-13 to 7.9395323e-13
Outputs:
- loss: float32 [], replicated
- grad_norm: float32 [], replicated
- new_patch: float32 [256, 768], P('dp')
- new_qkv: float32 [768, 2304], P('dp')
- new_out: float32 [768, 768], P('dp')
- new_up: float32 [768, 3072], P('dp')
- new_down: float32 [3072, 768], P('dp')
- new_proj: float32 [768, 1024], P('dp')
- new_gains: float32 [3, 768], P(None, 'dp')
- first_patch: float32 [256, 768], P('dp')
- first_qkv: float32 [768, 2304], P('dp')
- first_out: float32 [768, 768], P('dp')
- first_up: float32 [768, 3072], P('dp')
- first_down: float32 [3072, 768], P('dp')
- first_proj: float32 [768, 1024], P('dp')
- first_gains: float32 [3, 768], P(None, 'dp')
- second_patch: float32 [256, 768], P('dp')
- second_qkv: float32 [768, 2304], P('dp')
- second_out: float32 [768, 768], P('dp')
- second_up: float32 [768, 3072], P('dp')
- second_down: float32 [3072, 768], P('dp')
- second_proj: float32 [768, 1024], P('dp')
- second_gains: float32 [3, 768], P(None, 'dp')
Inputs may be any that keep to these rules, and one draw needn't show every extreme that they name: `clip_lengths`: each clip has 228 or 114 patches; in every micro-batch the first clip has 228 and the second 228 // 2.
All inputs are finite; a program needn't handle non-finite values.
Results may differ from a plain program's by a relative error of at most 0.014.
Values may be sent and summed in bfloat16 or wider, within the bound.
No kernel may reach another device: no remote copies, remote signals or barrier semaphores. Data moves between devices by JAX's collectives and lax.ppermute only.
A program may use at most 256 MiB of HBM per device.

v0:
```python
import jax
import jax.numpy as jnp
from jax import lax
from jax.sharding import PartitionSpec as P

HEADS_A = 12
HEADS_I = 16
LEN = 228
IMG_LEN = 256
MICRO = 2
STEP = 7
HIGHEST = lax.Precision.HIGHEST
NORM_EPS = 1e-06
LOGIT_SCALE = 50.0
CLIP_NORM = 0.01
BETA_ONE = 0.9
BETA_TWO = 0.999
ADAM_EPS = 1e-08
WEIGHT_DECAY = 0.1
RATE_MATRIX = 0.05
RATE_GAIN = 0.3


def to_low(value_in):
    return value_in.astype(jnp.bfloat16)


def normed(resid, gain):
    center = resid - jnp.mean(resid, axis=-1, keepdims=True)
    spread = jnp.mean(center * center, axis=-1, keepdims=True)
    return center * lax.rsqrt(spread + NORM_EPS) * gain


def unit_rows(embed_raw):
    return embed_raw * lax.rsqrt(jnp.sum(embed_raw * embed_raw, axis=-1, keepdims=True) + NORM_EPS)


def matmul(left, right):
    return jnp.einsum("cld,de->cle", left, right, preferred_element_type=jnp.float32)


def matmul_back(left, right):
    return jnp.einsum("cle,de->cld", left, right, preferred_element_type=jnp.float32)


def outer_sum(left, right):
    return jnp.einsum("cld,cle->de", left, right, preferred_element_type=jnp.float32)


def attend(query, keyed, valid, score_scale):
    scores = (
        jnp.einsum("clhd,cmhd->chlm", query, keyed, preferred_element_type=jnp.float32)
        * score_scale
    )
    return jnp.where(valid[:, None, None, :], scores, -1e30)


def layer_forward(resid_in, weights, norm_gains, valid, heads):
    w_qkv, w_out, w_up, w_down = weights
    clip_count, length, feature = resid_in.shape
    head_dim = feature // heads
    h_one = to_low(normed(resid_in, norm_gains[0]))
    qkv = to_low(matmul(h_one, w_qkv)).reshape(clip_count, length, 3, heads, head_dim)
    scores = attend(qkv[:, :, 0], qkv[:, :, 1], valid, head_dim ** (-0.5))
    log_total = jax.nn.logsumexp(scores, axis=-1, keepdims=True)
    attn_probs = jnp.exp(scores - log_total)
    attn_mixed = jnp.einsum(
        "chlm,cmhd->clhd", to_low(attn_probs), qkv[:, :, 2], preferred_element_type=jnp.float32
    )
    attn_mixed = to_low(attn_mixed.reshape(clip_count, length, feature))
    resid_mid = resid_in + matmul(attn_mixed, w_out)
    h_two = to_low(normed(resid_mid, norm_gains[1]))
    pre_act = matmul(h_two, w_up)
    hidden = to_low(jax.nn.gelu(pre_act))
    resid_out = resid_mid + matmul(hidden, w_down)
    return (
        resid_out,
        (h_one, qkv, log_total, attn_mixed, resid_mid, h_two, pre_act, hidden, resid_out),
    )


def pool_embed(resid_out, gain, pool_weight, w_proj):
    pooled = jnp.sum(normed(resid_out, gain) * pool_weight[:, :, None], axis=1)
    embed_raw = jnp.dot(to_low(pooled), w_proj, preferred_element_type=jnp.float32)
    return (unit_rows(embed_raw), pooled, embed_raw)


def contrast(audio, image, ids):
    logits = jnp.dot(audio, image.T, precision=HIGHEST) * LOGIT_SCALE
    count_rows = ids.shape[0]
    same = jnp.arange(count_rows)[:, None] == jnp.arange(count_rows)[None, :]
    allowed = jnp.logical_or(ids[:, None] != ids[None, :], same)
    masked = jnp.where(allowed, logits, -1e30)
    matched = jnp.sum(jnp.where(same, logits, 0.0), axis=1)
    row_lse = jax.nn.logsumexp(masked, axis=1)
    col_lse = jax.nn.logsumexp(masked, axis=0)
    return jnp.sum(row_lse - matched) + jnp.sum(col_lse - matched)


def audio_backward(
    d_embed, patches, resid_in, kept, pooled, embed_raw, weights, norm_gains, valid, pool_weight
):
    w_patch, w_qkv, w_out, w_up, w_down, w_proj = weights
    h_one, qkv, log_total, attn_mixed, resid_mid, h_two, pre_act, hidden, resid_out = kept
    clip_count, length, feature = resid_in.shape
    head_dim = feature // HEADS_A
    score_scale = head_dim ** (-0.5)
    d_raw = to_low(jax.vjp(unit_rows, embed_raw)[1](d_embed)[0])
    g_proj = jnp.dot(to_low(pooled).T, d_raw, preferred_element_type=jnp.float32)
    d_pooled = jnp.dot(d_raw, w_proj.T, preferred_element_type=jnp.float32)
    d_normed = d_pooled[:, None, :] * pool_weight[:, :, None]
    d_out, g_three = jax.vjp(normed, resid_out, norm_gains[2])[1](d_normed)
    d_low = to_low(d_out)
    g_down = outer_sum(hidden, d_low)
    d_hidden = matmul_back(d_low, w_down)
    d_pre = to_low(jax.vjp(jax.nn.gelu, pre_act)[1](d_hidden)[0])
    g_up = outer_sum(h_two, d_pre)
    d_ln_two, g_two = jax.vjp(normed, resid_mid, norm_gains[1])[1](matmul_back(d_pre, w_up))
    d_mid = d_out + d_ln_two
    d_mid_low = to_low(d_mid)
    g_out = outer_sum(attn_mixed, d_mid_low)
    d_mixed = to_low(matmul_back(d_mid_low, w_out)).reshape(clip_count, length, HEADS_A, head_dim)
    query, keyed, values_h = (qkv[:, :, 0], qkv[:, :, 1], qkv[:, :, 2])
    attn_probs = jnp.exp(attend(query, keyed, valid, score_scale) - log_total)
    d_probs = jnp.einsum("clhd,cmhd->chlm", d_mixed, values_h, preferred_element_type=jnp.float32)
    d_values = jnp.einsum(
        "chlm,clhd->cmhd", to_low(attn_probs), d_mixed, preferred_element_type=jnp.float32
    )
    d_scores = to_low(
        attn_probs * (d_probs - jnp.sum(attn_probs * d_probs, axis=-1, keepdims=True))
    )
    d_query = (
        jnp.einsum("chlm,cmhd->clhd", d_scores, keyed, preferred_element_type=jnp.float32)
        * score_scale
    )
    d_keyed = (
        jnp.einsum("chlm,clhd->cmhd", d_scores, query, preferred_element_type=jnp.float32)
        * score_scale
    )
    d_qkv = to_low(
        jnp.stack([d_query, d_keyed, d_values], axis=2).reshape(clip_count, length, 3 * feature)
    )
    g_qkv = outer_sum(h_one, d_qkv)
    d_ln_one, g_one = jax.vjp(normed, resid_in, norm_gains[0])[1](matmul_back(d_qkv, w_qkv))
    d_in = to_low(d_mid + d_ln_one)
    g_patch = outer_sum(patches, d_in)
    return (g_patch, g_qkv, g_out, g_up, g_down, g_proj, jnp.stack([g_one, g_two, g_three]))


def adam_step(weight, gradient, moment_one, moment_two, step_rate, decay):
    first_new = BETA_ONE * moment_one + (1.0 - BETA_ONE) * gradient
    second_new = BETA_TWO * moment_two + (1.0 - BETA_TWO) * gradient * gradient
    fixed_one = first_new / (1.0 - BETA_ONE**STEP)
    fixed_two = second_new / (1.0 - BETA_TWO**STEP)
    update = fixed_one / (jnp.sqrt(fixed_two) + ADAM_EPS) + decay * weight
    return (weight - step_rate * update, first_new, second_new)


def local(
    audio_patches,
    clip_lengths,
    video_ids,
    image_tokens,
    i_qkv,
    i_out,
    i_up,
    i_down,
    i_proj,
    i_gains,
    a_patch,
    a_qkv,
    a_out,
    a_up,
    a_down,
    a_proj,
    a_gains,
    m_patch,
    m_qkv,
    m_out,
    m_up,
    m_down,
    m_proj,
    m_gains,
    s_patch,
    s_qkv,
    s_out,
    s_up,
    s_down,
    s_proj,
    s_gains,
):
    masters = (a_patch, a_qkv, a_out, a_up, a_down, a_proj, a_gains)
    firsts = (m_patch, m_qkv, m_out, m_up, m_down, m_proj, m_gains)
    seconds = (s_patch, s_qkv, s_out, s_up, s_down, s_proj, s_gains)
    all_ids = lax.all_gather(video_ids, ("dp", "rep"), axis=1, tiled=True)
    image_w = (
        lax.all_gather(i_qkv, "dp", axis=0, tiled=True),
        lax.all_gather(i_out, "dp", axis=0, tiled=True),
        lax.all_gather(i_up, "dp", axis=0, tiled=True),
        lax.all_gather(i_down, "dp", axis=0, tiled=True),
        lax.all_gather(i_proj, "dp", axis=0, tiled=True),
        lax.all_gather(i_gains, "dp", axis=1, tiled=True),
    )
    image_g = image_w[5].astype(jnp.float32)
    count_rows = all_ids.shape[1]
    same = jnp.arange(count_rows)[:, None] == jnp.arange(count_rows)[None, :]
    allowed = jnp.logical_or(all_ids[:, :, None] != all_ids[:, None, :], same[None])
    loss_scale = count_rows / jnp.sum(allowed.astype(jnp.float32))
    copies = tuple((to_low(w) for w in masters))
    clip_dev = audio_patches.shape[1]
    start_row = lax.axis_index(("dp", "rep")) * clip_dev
    image_valid = jnp.ones((clip_dev, IMG_LEN), dtype=bool)
    image_pool = jnp.ones((clip_dev, IMG_LEN), jnp.float32) / IMG_LEN
    positions = jnp.arange(LEN)
    loss_sum = 0.0
    accum = None
    for micro in range(MICRO):
        gathered = (
            lax.all_gather(copies[0], "dp", axis=0, tiled=True),
            lax.all_gather(copies[1], "dp", axis=0, tiled=True),
            lax.all_gather(copies[2], "dp", axis=0, tiled=True),
            lax.all_gather(copies[3], "dp", axis=0, tiled=True),
            lax.all_gather(copies[4], "dp", axis=0, tiled=True),
            lax.all_gather(copies[5], "dp", axis=0, tiled=True),
            lax.all_gather(copies[6], "dp", axis=1, tiled=True),
        )
        gains_now = gathered[6].astype(jnp.float32)
        lengths_now = clip_lengths[micro]
        valid = positions[None, :] < lengths_now[:, None]
        pool_weight = valid.astype(jnp.float32) / lengths_now[:, None].astype(jnp.float32)
        patches = audio_patches[micro]
        resid_in = matmul(patches, gathered[0])
        resid_out, kept = layer_forward(resid_in, gathered[1:5], gains_now, valid, HEADS_A)
        audio_embed, pooled, embed_raw = pool_embed(
            resid_out, gains_now[2], pool_weight, gathered[5]
        )
        image_out, unused = layer_forward(
            image_tokens[micro].astype(jnp.float32), image_w[:4], image_g, image_valid, HEADS_I
        )
        image_embed, unused_pool, unused_raw = pool_embed(
            image_out, image_g[2], image_pool, image_w[4]
        )
        audio_all, image_all = (
            lax.all_gather(to_low(audio_embed), ("dp", "rep"), axis=0, tiled=True),
            lax.all_gather(to_low(image_embed), ("dp", "rep"), axis=0, tiled=True),
        )
        image_full = image_all.astype(jnp.float32)
        ids_now = all_ids[micro]

        def micro_loss(audio_in):
            return contrast(audio_in, image_full, ids_now)

        part_loss, contrast_back = jax.vjp(micro_loss, audio_all.astype(jnp.float32))
        loss_sum = loss_sum + part_loss
        d_all = contrast_back(loss_scale)[0]
        d_embed = lax.dynamic_slice_in_dim(d_all, start_row, clip_dev, 0)
        back_weights = (
            lax.all_gather(copies[0], "dp", axis=0, tiled=True),
            lax.all_gather(copies[1], "dp", axis=0, tiled=True),
            lax.all_gather(copies[2], "dp", axis=0, tiled=True),
            lax.all_gather(copies[3], "dp", axis=0, tiled=True),
            lax.all_gather(copies[4], "dp", axis=0, tiled=True),
            lax.all_gather(copies[5], "dp", axis=0, tiled=True),
            lax.all_gather(copies[6], "dp", axis=1, tiled=True),
        )
        grads = audio_backward(
            d_embed,
            patches,
            resid_in,
            kept,
            pooled,
            embed_raw,
            back_weights[:6],
            gains_now,
            valid,
            pool_weight,
        )
        shards = (
            lax.psum_scatter(grads[0], "dp", scatter_dimension=0, tiled=True),
            lax.psum_scatter(grads[1], "dp", scatter_dimension=0, tiled=True),
            lax.psum_scatter(grads[2], "dp", scatter_dimension=0, tiled=True),
            lax.psum_scatter(grads[3], "dp", scatter_dimension=0, tiled=True),
            lax.psum_scatter(grads[4], "dp", scatter_dimension=0, tiled=True),
            lax.psum_scatter(grads[5], "dp", scatter_dimension=0, tiled=True),
            lax.psum_scatter(grads[6], "dp", scatter_dimension=1, tiled=True),
        )
        accum = shards if accum is None else tuple((a + b for a, b in zip(accum, shards)))
    summed = lax.psum(accum, "rep")
    local_squares = sum((jnp.sum(g * g) for g in summed))
    grad_norm = jnp.sqrt(lax.psum(local_squares, "dp"))
    factor = jnp.minimum(1.0, CLIP_NORM / grad_norm)
    results = []
    for index in range(7):
        step_rate = RATE_GAIN if index == 6 else RATE_MATRIX
        decay = 0.0 if index == 6 else WEIGHT_DECAY
        results.append(
            adam_step(
                masters[index],
                summed[index] * factor,
                firsts[index],
                seconds[index],
                step_rate,
                decay,
            )
        )
    new_w = tuple((r[0] for r in results))
    new_one = tuple((r[1] for r in results))
    new_two = tuple((r[2] for r in results))
    loss = loss_sum * loss_scale
    return (
        loss,
        grad_norm,
        new_w[0],
        new_w[1],
        new_w[2],
        new_w[3],
        new_w[4],
        new_w[5],
        new_w[6],
        new_one[0],
        new_one[1],
        new_one[2],
        new_one[3],
        new_one[4],
        new_one[5],
        new_one[6],
        new_two[0],
        new_two[1],
        new_two[2],
        new_two[3],
        new_two[4],
        new_two[5],
        new_two[6],
    )


def solution(mesh):
    placed = (
        P(None, ("dp", "rep"), None, None),
        P(None, ("dp", "rep")),
        P(None, ("dp", "rep")),
        P(None, ("dp", "rep"), None, None),
        P("dp", None),
        P("dp", None),
        P("dp", None),
        P("dp", None),
        P("dp", None),
        P(None, "dp"),
        P("dp", None),
        P("dp", None),
        P("dp", None),
        P("dp", None),
        P("dp", None),
        P("dp", None),
        P(None, "dp"),
        P("dp", None),
        P("dp", None),
        P("dp", None),
        P("dp", None),
        P("dp", None),
        P("dp", None),
        P(None, "dp"),
        P("dp", None),
        P("dp", None),
        P("dp", None),
        P("dp", None),
        P("dp", None),
        P("dp", None),
        P(None, "dp"),
    )
    return jax.shard_map(
        local,
        mesh=mesh,
        in_specs=placed,
        out_specs=(
            P(),
            P(),
            P("dp", None),
            P("dp", None),
            P("dp", None),
            P("dp", None),
            P("dp", None),
            P("dp", None),
            P(None, "dp"),
            P("dp", None),
            P("dp", None),
            P("dp", None),
            P("dp", None),
            P("dp", None),
            P("dp", None),
            P(None, "dp"),
            P("dp", None),
            P("dp", None),
            P("dp", None),
            P("dp", None),
            P("dp", None),
            P("dp", None),
            P(None, "dp"),
        ),
        check_vma=False,
    )
```

profile of v0, /device:TPU:0, one launch (start us, length us, event | category | flops | bytes accessed | tf_op | source)
XLA Modules:
  0.0 1388.9 jit_solution(7028372803511178560)
XLA Ops:
  17.8 12.7 all_gather.72
  31.3 8.8 all-gather.1
  43.6 8.1 all-gather.3
  55.1 68.0 %all-gather = s32[32,2,2]{2,1,0:T(2,128)S(1)} all-gather(s32[1,2,2]{2,1,0:T(2,128)S(1)} %bitcast.448), channel_id=1, replica_groups=mesh['dp'=8,'rep'=4] {'dp','rep'}, dimensions={0}, use_global_device_ids=true | all-gather | bytes 528 | tf_op jit(solution)/shard_map/all_gather | solution.py:195
  125.9 5.5 convolution_convert_fusion
  166.4 7.4 fusion.76
  173.8 7.2 fusion.338
  190.0 67.5 %all-gather.2 = bf16[32,2,1024]{2,1,0:T(2,128)(2,1)S(1)} all-gather(bf16[1,2,1024]{2,1,0:T(2,128)(2,1)S(1)} %fusion.251), channel_id=1, replica_groups=mesh['dp'=8,'rep'=4] {'dp','rep'}, dimensions={0}, use_global_device_ids=true | all-gather | bytes 135168 | tf_op jit(solution)/shard_map/all_gather | solution.py:244
  257.6 11.4 fusion.28
  269.0 6.4 copy.271
  291.6 12.1 fusion.31
  303.7 6.5 copy.284
  322.3 37.6 %all-gather.32.cloned.1.call-done = bf16[1280,5120]{1,0:T(8,128)(2,1)} async-done(((bf16[160,5120]{1,0:T(8,128)(2,1)}), bf16[1280,5120]{1,0:T(8,128)(2,1)}) %all-gather.32.cloned.1.call-update) | async-done | bytes 13107216 | tf_op jit(solution)/shard_map/all_gather | solution.py:199
  359.9 76.3 %all-gather.34.cloned.1.call-done = bf16[5120,1280]{1,0:T(8,128)(2,1)} async-done(((bf16[640,1280]{1,0:T(8,128)(2,1)}), bf16[5120,1280]{1,0:T(8,128)(2,1)}) %all-gather.34.cloned.1.call-update) | async-done | bytes 13107216 | tf_op jit(solution)/shard_map/all_gather | solution.py:200
  436.2 26.1 %fusion.333 = (f32[2,256]{1,0:T(2,128)S(1)}, f32[2,256,1280]{2,1,0:T(8,128)}) fusion(f32[2,256,1280]{2,1,0:T(8,128)} %copy-done.26, bf16[5120,1280]{1,0:T(8,128)(2,1)} %all-gather.34.cloned.1.call-done, bf16[1280,5120]{1,0:T(8,128)(2,1)} %all-gather.32.cloned.1.call-done, f32[1280]{0:T(1024)S(1)} %get-tuple-element.142, f32[2,256]{1,0:T(2,128)S(1)} %add_rsqrt_fusion.4, ...), kind=kOutput, calls=%fused_computation.521 | convolution fusion | flops 13449297920 | bytes 31468544 | tf_op jit(solution)/shard_map/cld,de->cle/dot_general | solution.py:39
  464.5 26.0 %fusion.329 = (f32[2,256]{1,0:T(2,128)S(1)}, f32[2,256,1280]{2,1,0:T(8,128)}) fusion(f32[2,256,1280]{2,1,0:T(8,128)} %copy-done.27, bf16[5120,1280]{1,0:T(8,128)(2,1)} %all-gather.34.cloned.1.call-done, bf16[1280,5120]{1,0:T(8,128)(2,1)} %all-gather.32.cloned.1.call-done, f32[2,256]{1,0:T(2,128)S(1)} %add_rsqrt_fusion.1, ...), kind=kOutput, calls=%fused_computation.519 | convolution fusion | flops 13449297920 | bytes 31468544 | tf_op jit(solution)/shard_map/cld,de->cle/dot_general | solution.py:39
  498.2 68.3 %all-gather.4 = bf16[32,2,1024]{2,1,0:T(2,128)(2,1)S(1)} all-gather(bf16[1,2,1024]{2,1,0:T(2,128)(2,1)S(1)} %fusion.252), channel_id=1, replica_groups=mesh['dp'=8,'rep'=4] {'dp','rep'}, dimensions={0}, use_global_device_ids=true | all-gather | bytes 135168 | tf_op jit(solution)/shard_map/all_gather | solution.py:245
  573.1 64.3 %all-gather.6 = bf16[32,2,1024]{2,1,0:T(2,128)(2,1)S(1)} all-gather(bf16[1,2,1024]{2,1,0:T(2,128)(2,1)S(1)} %fusion.254), channel_id=1, replica_groups=mesh['dp'=8,'rep'=4] {'dp','rep'}, dimensions={0}, use_global_device_ids=true | all-gather | bytes 135168 | tf_op jit(solution)/shard_map/all_gather | solution.py:245
  638.0 66.8 %all-gather.5 = bf16[32,2,1024]{2,1,0:T(2,128)(2,1)S(1)} all-gather(bf16[1,2,1024]{2,1,0:T(2,128)(2,1)S(1)} %fusion.253), channel_id=1, replica_groups=mesh['dp'=8,'rep'=4] {'dp','rep'}, dimensions={0}, use_global_device_ids=true | all-gather | bytes 135168 | tf_op jit(solution)/shard_map/all_gather | solution.py:244
  709.8 8.7 fusion.40
  718.6 8.8 fusion.47
  806.6 6.6 fusion.193
  813.2 9.9 bitcast_add_fusion
  835.9 29.7 %reduce-scatter.14.cloned.1.call-done = f32[96,768]{1,0:T(8,128)} async-done(((f32[768,768]{1,0:T(8,128)}), f32[96,768]{1,0:T(8,128)}) %reduce-scatter.14.cloned.1.call-update) | async-done | bytes 294928 | tf_op jit(solution)/shard_map/reduce_scatter | solution.py:281
  865.6 50.0 %reduce-scatter.20.cloned.1.call-done = f32[96,1024]{1,0:T(8,128)} async-done(((f32[768,1024]{1,0:T(8,128)}), f32[96,1024]{1,0:T(8,128)}) %reduce-scatter.20.cloned.1.call-update) | async-done | bytes 393232 | tf_op jit(solution)/shard_map/reduce_scatter | solution.py:284
  915.6 68.9 %reduce-scatter.12.cloned.1.call-done = f32[96,2304]{1,0:T(8,128)} async-done(((f32[768,2304]{1,0:T(8,128)}), f32[96,2304]{1,0:T(8,128)}) %reduce-scatter.12.cloned.1.call-update) | async-done | bytes 884752 | tf_op jit(solution)/shard_map/reduce_scatter | solution.py:280
  984.5 80.3 %reduce-scatter.18.cloned.1.call-done = f32[384,768]{1,0:T(8,128)} async-done(((f32[3072,768]{1,0:T(8,128)}), f32[384,768]{1,0:T(8,128)}) %reduce-scatter.18.cloned.1.call-update) | async-done | bytes 1179664 | tf_op jit(solution)/shard_map/reduce_scatter | solution.py:283
  1064.8 80.3 %reduce-scatter.16.cloned.1.call-done = f32[96,3072]{1,0:T(8,128)} async-done(((f32[768,3072]{1,0:T(8,128)}), f32[96,3072]{1,0:T(8,128)}) %reduce-scatter.16.cloned.1.call-update) | async-done | bytes 1179664 | tf_op jit(solution)/shard_map/reduce_scatter | solution.py:282
  1147.8 34.9 %reduce-scatter.24.cloned.1.call-done = f32[96,3]{1,0:T(8,128)} async-done(((f32[768,3]{1,0:T(8,128)}), f32[96,3]{1,0:T(8,128)}) %reduce-scatter.24.cloned.1.call-update) | async-done | bytes 1168
  1183.6 12.2 psum.62
  1196.3 140.8 %all-reduce.3.cloned.1.call-done = (f32[32,768]{1,0:T(8,128)}, f32[96,2304]{1,0:T(8,128)}, f32[96,768]{1,0:T(8,128)}, f32[96,3072]{1,0:T(8,128)}, f32[384,768]{1,0:T(8,128)}, /*index=5*/f32[96,1024]{1,0:T(8,128)}) async-done(((f32[32,768]{1,0:T(8,128)}, f32[96,2304]{1,0:T(8,128)}, f32[96,768]{1,0:T(8,128)}, f32[96,3072]{1,0:T(8,128)}, f32[384,768]{1,0:T(8,128)}, /*index=5*/f32[96,1024]{1,0:T(8,128)}), ...) | async-done | bytes 4030480 | tf_op jit(solution)/shard_map/psum | solution.py:288
  1350.7 14.2 %psum.63 = f32[]{:T(128)} all-reduce(f32[]{:T(128)S(6)} %add.527), channel_id=1, replica_groups=mesh['dp'=8,'rep'=4] {'dp'}, use_global_device_ids=true, to_apply=%region_105.106 | all-reduce | flops 1 | bytes 8 | tf_op jit(solution)/shard_map/psum | solution.py:290
  (545 shorter events, 229.0 us)
Async XLA Ops:
  7.2 118.6 %all-gather.18.cloned.1.call-start = ((), (), s32[]{:S(2)}) async-start(), calls=%async_computation.7 | async-start | bytes 3981312 | tf_op jit(solution)/shard_map/all_gather | solution.py:220
  9.4 135.7 %all-gather.20.cloned.1.call-start = ((), (), s32[]{:S(2)}) async-start(), calls=%async_computation.8 | async-start | bytes 1327104 | tf_op jit(solution)/shard_map/all_gather | solution.py:221
  11.1 155.2 %all-gather.22.cloned.1.call-start = ((), (), s32[]{:S(2)}) async-start(), calls=%async_computation.9 | async-start | bytes 5308416 | tf_op jit(solution)/shard_map/all_gather | solution.py:222
  12.1 161.7 %all-gather.24.cloned.1.call-start = ((), (), s32[]{:S(2)}) async-start(), calls=%async_computation.10 | async-start | bytes 5308416 | tf_op jit(solution)/shard_map/all_gather | solution.py:223
  13.1 175.0 %all-gather.26.cloned.1.call-start = ((), (), s32[]{:S(2)}) async-start(), calls=%async_computation.11 | async-start | bytes 1769472 | tf_op jit(solution)/shard_map/all_gather | solution.py:224
  13.9 243.7 %all-gather.28.cloned.1.call-start = ((), (), s32[]{:S(2)}) async-start(), calls=%async_computation.12 | async-start | bytes 11059200 | tf_op jit(solution)/shard_map/all_gather | solution.py:197
  14.4 269.7 %all-gather.30.cloned.1.call-start = ((), (), s32[]{:S(2)}) async-start(), calls=%async_computation.13 | async-start | bytes 3686400 | tf_op jit(solution)/shard_map/all_gather | solution.py:198
  15.2 344.7 %all-gather.32.cloned.1.call-start = ((), (), s32[]{:S(2)}) async-start(), calls=%async_computation.14 | async-start | bytes 14745600 | tf_op jit(solution)/shard_map/all_gather | solution.py:199
  16.0 420.2 %all-gather.34.cloned.1.call-start = ((), (), s32[]{:S(2)}) async-start(), calls=%async_computation.15 | async-start | bytes 14745600 | tf_op jit(solution)/shard_map/all_gather | solution.py:200
  16.7 479.1 %all-gather.36.cloned.1.call-start = ((), (), s32[]{:S(2)}) async-start(), calls=%async_computation.16 | async-start | bytes 2949120 | tf_op jit(solution)/shard_map/all_gather | solution.py:201
  17.3 818.6 %reduce-scatter.22.cloned.1.call-start = ((), (), s32[]{:S(2)}) async-start(), calls=%async_computation.22 | async-start | bytes 884736 | tf_op jit(solution)/shard_map/reduce_scatter | solution.py:279
  31.0 114.1 %copy-start.4 = (f32[2,228,768]{2,1,0:T(8,128)}, f32[2,228,768]{2,1,0:T(8,128)S(1)}, u32[]{:S(2)}) copy-start(f32[2,228,768]{2,1,0:T(8,128)S(1)} %get-tuple-element.230) | copy-start | bytes 4202500
  31.0 94.9 %copy-start.109 = (f32[2,228]{1,0:T(2,128)}, f32[2,228]{1,0:T(2,128)S(1)}, u32[]{:S(2)}) copy-start(f32[2,228]{1,0:T(2,128)S(1)} %broadcast_multiply_fusion.8) | copy-start | bytes 5476
  31.3 94.6 %copy-start.125 = (f32[2,228]{1,0:T(2,128)}, f32[2,228]{1,0:T(2,128)S(1)}, u32[]{:S(2)}) copy-start(f32[2,228]{1,0:T(2,128)S(1)} %fusion.266) | copy-start | bytes 5476
  40.2 107.7 %copy-start.93 = (f32[768]{0:T(1024)}, f32[768]{0:T(1024)S(1)}, u32[]{:S(2)}) copy-start(f32[768]{0:T(1024)S(1)} %get-tuple-element.146) | copy-start | bytes 9220
  40.2 141.0 %copy-start.63 = (f32[768]{0:T(1024)}, f32[768]{0:T(1024)S(1)}, u32[]{:S(2)}) copy-start(f32[768]{0:T(1024)S(1)} %get-tuple-element.145) | copy-start | bytes 9220
  52.9 95.1 %copy-start.106 = (f32[2,228]{1,0:T(2,128)}, f32[2,228]{1,0:T(2,128)S(1)}, u32[]{:S(2)}) copy-start(f32[2,228]{1,0:T(2,128)S(1)} %broadcast_multiply_fusion.11) | copy-start | bytes 5476
  54.3 93.7 %copy-start.115 = (f32[2,228]{1,0:T(2,128)}, f32[2,228]{1,0:T(2,128)S(1)}, u32[]{:S(2)}) copy-start(f32[2,228]{1,0:T(2,128)S(1)} %fusion.263) | copy-start | bytes 5476
  54.9 105.3 %copy-start.102 = (pred[2,228]{1,0:T(4,128)(4,1)}, pred[2,228]{1,0:T(4,128)(4,1)S(1)}, u32[]{:S(2)}) copy-start(pred[2,228]{1,0:T(4,128)(4,1)S(1)} %get-tuple-element.251) | copy-start | bytes 1372
  187.4 383.8 %copy-start.7 = (f32[2,228,768]{2,1,0:T(8,128)}, f32[2,228,768]{2,1,0:T(8,128)S(1)}, u32[]{:S(2)}) copy-start(f32[2,228,768]{2,1,0:T(8,128)S(1)} %get-tuple-element.211) | copy-start | bytes 4202500
  572.5 132.4 %copy-start.113 = (s32[64]{0:T(128)S(1)}, s32[64]{0:T(128)}, u32[]{:S(2)}) copy-start(s32[64]{0:T(128)} %get-tuple-element.194) | copy-start | bytes 772
  787.3 78.3 %reduce-scatter.14.cloned.1.call-start = ((), (), s32[]{:S(2)}) async-start(), calls=%async_computation.18 | async-start | bytes 2654208 | tf_op jit(solution)/shard_map/reduce_scatter | solution.py:281
  791.9 123.7 %reduce-scatter.20.cloned.1.call-start = ((), (), s32[]{:S(2)}) async-start(), calls=%async_computation.21 | async-start | bytes 3538944 | tf_op jit(solution)/shard_map/reduce_scatter | solution.py:284
  796.2 188.3 %reduce-scatter.12.cloned.1.call-start = ((), (), s32[]{:S(2)}) async-start(), calls=%async_computation.17 | async-start | bytes 7962624 | tf_op jit(solution)/shard_map/reduce_scatter | solution.py:280
  806.3 258.6 %reduce-scatter.18.cloned.1.call-start = ((), (), s32[]{:S(2)}) async-start(), calls=%async_computation.20 | async-start | bytes 10616832 | tf_op jit(solution)/shard_map/reduce_scatter | solution.py:283
  823.1 322.0 %reduce-scatter.16.cloned.1.call-start = ((), (), s32[]{:S(2)}) async-start(), calls=%async_computation.19 | async-start | bytes 10616832 | tf_op jit(solution)/shard_map/reduce_scatter | solution.py:282
  834.7 348.0 %reduce-scatter.24.cloned.1.call-start = ((), (), s32[]{:S(2)}) async-start(), calls=%async_computation.23 | async-start | bytes 442368
  835.8 501.3 %all-reduce.3.cloned.1.call-start = ((), (), s32[]{:S(2)}) async-start(), calls=%async_computation.24 | async-start | bytes 8060928 | tf_op jit(solution)/shard_map/psum | solution.py:288
  1145.1 220.5 %copy-start.128 = (f32[3,96]{1,0:T(4,128)S(1)}, f32[3,96]{1,0:T(4,128)}, u32[]{:S(2)}) copy-start(f32[3,96]{1,0:T(4,128)} %param.47) | copy-start | bytes 3460
  1145.1 220.5 %copy-start.130 = (f32[3,96]{1,0:T(4,128)S(1)}, f32[3,96]{1,0:T(4,128)}, u32[]{:S(2)}) copy-start(f32[3,96]{1,0:T(4,128)} %param.54) | copy-start | bytes 3460
  1145.1 220.5 %copy-start.131 = (f32[3,96]{1,0:T(4,128)S(1)}, f32[3,96]{1,0:T(4,128)}, u32[]{:S(2)}) copy-start(f32[3,96]{1,0:T(4,128)} %param.61) | copy-start | bytes 3460
  1145.2 221.1 %copy-start.61 = (f32[96,1024]{1,0:T(8,128)S(1)}, f32[96,1024]{1,0:T(8,128)}, u32[]{:S(2)}) copy-start(f32[96,1024]{1,0:T(8,128)} %param.46) | copy-start | bytes 1179652
  (133 other events, 982.9 us)
Sparse Core Ops, SparseCore 0:
  10.5 38.2 all-gather.17
  51.2 24.0 all-gather.19
  77.8 38.9 all-gather.21
  119.1 38.9 all-gather.23
  160.4 25.6 all-gather.25
  187.9 60.9 all-gather.27
  250.8 32.8 all-gather.29
  285.5 74.3 all-gather.31
  361.8 74.3 all-gather.33
  437.9 30.1 all-gather.35
  787.4 32.4 reduce-scatter.21
  823.1 42.4 reduce-scatter.13
  869.4 46.2 reduce-scatter.19
  919.0 65.5 reduce-scatter.11
  988.3 76.4 reduce-scatter.17
  1068.6 76.4 reduce-scatter.15
  1148.9 33.7 reduce-scatter.23
  1185.6 151.4 all-reduce.2
where the time goes:
time: 1400 us; the launch traced here: 1390 us
  waiting for transfers between devices  602 us (43%)
  blocking collectives  391 us (28%)
  matrix products  252 us (18%)
  other arithmetic  62.3 us (4%)
  local copies, waits for them, and re-layouts  53.3 us (4%)
  between operations  27.9 us (2%)
    psum x1, waiting for transfers between devices, local(): summed = lax.psum(accum, 'rep')  141 us
    all_gather x2, blocking collectives, local(): lax.all_gather(to_low(audio_embed), ('dp', 'rep'), axis=0, tiled=True)  134 us
    all_gather x2, blocking collectives, local(): lax.all_gather(to_low(image_embed), ('dp', 'rep'), axis=0, tiled=True)  133 us
    dot_general x16, matrix products, matmul(): jnp.einsum('cld,de->cle', left, right, preferred_element_type=jnp.float32)  116 us
    reduce_scatter x1, waiting for transfers between devices, local(): lax.psum_scatter(grads[3], 'dp', scatter_dimension=0, tiled=True)  80.3 us
    reduce_scatter x1, waiting for transfers between devices, local(): lax.psum_scatter(grads[4], 'dp', scatter_dimension=0, tiled=True)  80.3 us
    all_gather x1, waiting for transfers between devices, local(): lax.all_gather(i_down, 'dp', axis=0, tiled=True)  76.3 us
    reduce_scatter x1, waiting for transfers between devices, local(): lax.psum_scatter(grads[1], 'dp', scatter_dimension=0, tiled=True)  68.9 us
  transfers between devices with their start and end apart: 18, of which 9 were waited for; matrix products, arithmetic and copies ran while one was open for 17% of the time, Pallas kernels for 0%

commit v1 on v0

--- a/solution.py
+++ b/solution.py
@@ -19,6 +19,18 @@
 WEIGHT_DECAY = 0.1
 RATE_MATRIX = 0.05
 RATE_GAIN = 0.3
+
+
+def doubled_up(shard, axis, dim):
+    ways, here, step = (lax.axis_size(axis), lax.axis_index(axis), shard.shape[dim])
+    line, have = (shard, 1)
+    while have < ways:
+        line = jnp.concatenate(
+            [line, lax.ppermute(line, axis, [(d, (d - have) % ways) for d in range(ways)])],
+            axis=dim,
+        )
+        have = 2 * have
+    return jnp.roll(line, here * step, axis=dim)
 
 
 def to_low(value_in):
@@ -242,7 +254,7 @@
         )
         audio_all, image_all = (
             lax.all_gather(to_low(audio_embed), ("dp", "rep"), axis=0, tiled=True),
-            lax.all_gather(to_low(image_embed), ("dp", "rep"), axis=0, tiled=True),
+            doubled_up(to_low(image_embed), ("dp", "rep"), 0),
         )
         image_full = image_all.astype(jnp.float32)
         ids_now = all_ids[micro]

time: 1400 us -> 1350 us (0.964)
  blocking collectives: 391 us -> 258 us
  waiting for transfers between devices: 602 us -> 682 us
    all_gather x2 -> x0, blocking collectives: 133 us -> none  [local(): lax.all_gather(to_low(image_embed), ('dp', 'rep'), axis=0, tiled=True)]
    all_gather x1, waiting for transfers between devices: 0.02 us -> 58.2 us  [local(): lax.all_gather(i_qkv, 'dp', axis=0, tiled=True)]
  transfers between devices with their start and end apart: 18 -> 28, of which waited for: 9 -> 16; matrix products, arithmetic and copies ran while one was open for 17% -> 18% of each run, Pallas kernels for 0% -> 0%
where the time goes in v1:
time: 1350 us; the launch traced here: 1340 us
  waiting for transfers between devices  682 us (51%)
  blocking collectives  258 us (19%)
  matrix products  249 us (18%)
  other arithmetic  63.1 us (5%)
  local copies, waits for them, and re-layouts  52.7 us (4%)
  between operations  28.1 us (2%)
    psum x1, waiting for transfers between devices, local(): summed = lax.psum(accum, 'rep')  141 us
    all_gather x2, blocking collectives, local(): lax.all_gather(to_low(audio_embed), ('dp', 'rep'), axis=0, tiled=True)  134 us
    dot_general x16, matrix products, matmul(): jnp.einsum('cld,de->cle', left, right, preferred_element_type=jnp.float32)  116 us
    reduce_scatter x1, waiting for transfers between devices, local(): lax.psum_scatter(grads[3], 'dp', scatter_dimension=0, tiled=True)  80.3 us
    reduce_scatter x1, waiting for transfers between devices, local(): lax.psum_scatter(grads[4], 'dp', scatter_dimension=0, tiled=True)  80.3 us
    all_gather x1, waiting for transfers between devices, local(): lax.all_gather(i_down, 'dp', axis=0, tiled=True)  76.3 us
    reduce_scatter x1, waiting for transfers between devices, local(): lax.psum_scatter(grads[1], 'dp', scatter_dimension=0, tiled=True)  68.9 us
    all_gather x1, blocking collectives, local(): all_ids = lax.all_gather(video_ids, ('dp', 'rep'), axis=1, tiled=True)  68 us
  transfers between devices with their start and end apart: 28, of which 16 were waited for; matrix products, arithmetic and copies ran while one was open for 18% of the time, Pallas kernels for 0%

profile of v1, /device:TPU:0, one launch (start us, length us, event | category | flops | bytes accessed | tf_op | source)
XLA Modules:
  0.0 1343.2 jit_solution(3661724690624586458)
XLA Ops:
  17.8 12.7 all_gather.66
  31.3 8.8 all-gather.1
  43.7 8.0 all-gather.3
  55.1 68.0 %all-gather = s32[32,2,2]{2,1,0:T(2,128)S(1)} all-gather(s32[1,2,2]{2,1,0:T(2,128)S(1)} %bitcast.440), channel_id=1, replica_groups=mesh['dp'=8,'rep'=4] {'dp','rep'}, dimensions={0}, use_global_device_ids=true | all-gather | bytes 528 | tf_op jit(solution)/shard_map/all_gather | solution.py:207
  125.8 5.5 convolution_convert_fusion
  165.7 7.3 fusion.76
  173.0 7.6 fusion.342
  190.2 58.2 %all-gather.26.cloned.1.call-done = bf16[1280,3840]{1,0:T(8,128)(2,1)} async-done(((bf16[160,3840]{1,0:T(8,128)(2,1)}), bf16[1280,3840]{1,0:T(8,128)(2,1)}) %all-gather.26.cloned.1.call-update) | async-done | bytes 9830416 | tf_op jit(solution)/shard_map/all_gather | solution.py:209
  248.4 11.0 fusion.28
  259.4 6.4 copy.271
  274.6 8.6 all-gather.28.cloned.1.call-done
  290.7 12.1 fusion.31
  302.7 6.5 copy.284
  321.3 38.1 %all-gather.30.cloned.1.call-done = bf16[1280,5120]{1,0:T(8,128)(2,1)} async-done(((bf16[160,5120]{1,0:T(8,128)(2,1)}), bf16[1280,5120]{1,0:T(8,128)(2,1)}) %all-gather.30.cloned.1.call-update) | async-done | bytes 13107216 | tf_op jit(solution)/shard_map/all_gather | solution.py:211
  359.4 76.3 %all-gather.32.cloned.1.call-done = bf16[5120,1280]{1,0:T(8,128)(2,1)} async-done(((bf16[640,1280]{1,0:T(8,128)(2,1)}), bf16[5120,1280]{1,0:T(8,128)(2,1)}) %all-gather.32.cloned.1.call-update) | async-done | bytes 13107216 | tf_op jit(solution)/shard_map/all_gather | solution.py:212
  435.7 26.1 %fusion.337 = (f32[2,256]{1,0:T(2,128)S(1)}, f32[2,256,1280]{2,1,0:T(8,128)}) fusion(f32[2,256,1280]{2,1,0:T(8,128)} %copy-done.26, bf16[5120,1280]{1,0:T(8,128)(2,1)} %all-gather.32.cloned.1.call-done, bf16[1280,5120]{1,0:T(8,128)(2,1)} %all-gather.30.cloned.1.call-done, f32[1280]{0:T(1024)S(1)} %get-tuple-element.143, f32[2,256]{1,0:T(2,128)S(1)} %add_rsqrt_fusion.4, ...), kind=kOutput, calls=%fused_computation.531 | convolution fusion | flops 13449297920 | bytes 31468544 | tf_op jit(solution)/shard_map/cld,de->cle/dot_general | solution.py:51
  464.0 26.0 %fusion.333 = (f32[2,256]{1,0:T(2,128)S(1)}, f32[2,256,1280]{2,1,0:T(8,128)}) fusion(f32[2,256,1280]{2,1,0:T(8,128)} %copy-done.27, bf16[5120,1280]{1,0:T(8,128)(2,1)} %all-gather.32.cloned.1.call-done, bf16[1280,5120]{1,0:T(8,128)(2,1)} %all-gather.30.cloned.1.call-done, f32[2,256]{1,0:T(2,128)S(1)} %add_rsqrt_fusion.1, ...), kind=kOutput, calls=%fused_computation.529 | convolution fusion | flops 13449297920 | bytes 31468544 | tf_op jit(solution)/shard_map/cld,de->cle/dot_general | solution.py:51
  518.4 69.6 %all-gather.2 = bf16[32,2,1024]{2,1,0:T(2,128)(2,1)S(1)} all-gather(bf16[1,2,1024]{2,1,0:T(2,128)(2,1)S(1)} %fusion.253), channel_id=1, replica_groups=mesh['dp'=8,'rep'=4] {'dp','rep'}, dimensions={0}, use_global_device_ids=true | all-gather | bytes 135168 | tf_op jit(solution)/shard_map/all_gather | solution.py:256
  595.4 64.4 %all-gather.4 = bf16[32,2,1024]{2,1,0:T(2,128)(2,1)S(1)} all-gather(bf16[1,2,1024]{2,1,0:T(2,128)(2,1)S(1)} %fusion.254), channel_id=1, replica_groups=mesh['dp'=8,'rep'=4] {'dp','rep'}, dimensions={0}, use_global_device_ids=true | all-gather | bytes 135168 | tf_op jit(solution)/shard_map/all_gather | solution.py:256
  665.5 8.7 fusion.40
  674.3 5.6 fusion.47
  759.3 6.6 fusion.193
  765.9 9.9 bitcast_add_fusion
  788.6 31.4 %reduce-scatter.14.cloned.1.call-done = f32[96,768]{1,0:T(8,128)} async-done(((f32[768,768]{1,0:T(8,128)}), f32[96,768]{1,0:T(8,128)}) %reduce-scatter.14.cloned.1.call-update) | async-done | bytes 294928 | tf_op jit(solution)/shard_map/reduce_scatter | solution.py:293
  820.0 50.0 %reduce-scatter.20.cloned.1.call-done = f32[96,1024]{1,0:T(8,128)} async-done(((f32[768,1024]{1,0:T(8,128)}), f32[96,1024]{1,0:T(8,128)}) %reduce-scatter.20.cloned.1.call-update) | async-done | bytes 393232 | tf_op jit(solution)/shard_map/reduce_scatter | solution.py:296
  870.0 68.9 %reduce-scatter.12.cloned.1.call-done = f32[96,2304]{1,0:T(8,128)} async-done(((f32[768,2304]{1,0:T(8,128)}), f32[96,2304]{1,0:T(8,128)}) %reduce-scatter.12.cloned.1.call-update) | async-done | bytes 884752 | tf_op jit(solution)/shard_map/reduce_scatter | solution.py:292
  938.9 80.3 %reduce-scatter.18.cloned.1.call-done = f32[384,768]{1,0:T(8,128)} async-done(((f32[3072,768]{1,0:T(8,128)}), f32[384,768]{1,0:T(8,128)}) %reduce-scatter.18.cloned.1.call-update) | async-done | bytes 1179664 | tf_op jit(solution)/shard_map/reduce_scatter | solution.py:295
  1019.2 80.3 %reduce-scatter.16.cloned.1.call-done = f32[96,3072]{1,0:T(8,128)} async-done(((f32[768,3072]{1,0:T(8,128)}), f32[96,3072]{1,0:T(8,128)}) %reduce-scatter.16.cloned.1.call-update) | async-done | bytes 1179664 | tf_op jit(solution)/shard_map/reduce_scatter | solution.py:294
  1102.2 34.9 %reduce-scatter.24.cloned.1.call-done = f32[96,3]{1,0:T(8,128)} async-done(((f32[768,3]{1,0:T(8,128)}), f32[96,3]{1,0:T(8,128)}) %reduce-scatter.24.cloned.1.call-update) | async-done | bytes 1168
  1137.9 12.2 psum.62
  1150.7 140.8 %all-reduce.3.cloned.1.call-done = (f32[32,768]{1,0:T(8,128)}, f32[96,2304]{1,0:T(8,128)}, f32[96,768]{1,0:T(8,128)}, f32[96,3072]{1,0:T(8,128)}, f32[384,768]{1,0:T(8,128)}, /*index=5*/f32[96,1024]{1,0:T(8,128)}) async-done(((f32[32,768]{1,0:T(8,128)}, f32[96,2304]{1,0:T(8,128)}, f32[96,768]{1,0:T(8,128)}, f32[96,3072]{1,0:T(8,128)}, f32[384,768]{1,0:T(8,128)}, /*index=5*/f32[96,1024]{1,0:T(8,128)}), ...) | async-done | bytes 4030480 | tf_op jit(solution)/shard_map/psum | solution.py:300
  1305.1 14.2 %psum.63 = f32[]{:T(128)} all-reduce(f32[]{:T(128)S(6)} %add.537), channel_id=1, replica_groups=mesh['dp'=8,'rep'=4] {'dp'}, use_global_device_ids=true, to_apply=%region_105.107 | all-reduce | flops 1 | bytes 8 | tf_op jit(solution)/shard_map/psum | solution.py:302
  (581 shorter events, 250.3 us)
Async XLA Ops:
  7.2 118.6 %all-gather.16.cloned.1.call-start = ((), (), s32[]{:S(2)}) async-start(), calls=%async_computation.7 | async-start | bytes 3981312 | tf_op jit(solution)/shard_map/all_gather | solution.py:232
  9.4 135.0 %all-gather.18.cloned.1.call-start = ((), (), s32[]{:S(2)}) async-start(), calls=%async_computation.8 | async-start | bytes 1327104 | tf_op jit(solution)/shard_map/all_gather | solution.py:233
  11.1 154.5 %all-gather.20.cloned.1.call-start = ((), (), s32[]{:S(2)}) async-start(), calls=%async_computation.9 | async-start | bytes 5308416 | tf_op jit(solution)/shard_map/all_gather | solution.py:234
  12.1 160.9 %all-gather.22.cloned.1.call-start = ((), (), s32[]{:S(2)}) async-start(), calls=%async_computation.10 | async-start | bytes 5308416 | tf_op jit(solution)/shard_map/all_gather | solution.py:235
  13.1 174.4 %all-gather.24.cloned.1.call-start = ((), (), s32[]{:S(2)}) async-start(), calls=%async_computation.11 | async-start | bytes 1769472 | tf_op jit(solution)/shard_map/all_gather | solution.py:236
  13.9 234.5 %all-gather.26.cloned.1.call-start = ((), (), s32[]{:S(2)}) async-start(), calls=%async_computation.12 | async-start | bytes 11059200 | tf_op jit(solution)/shard_map/all_gather | solution.py:209
  14.4 268.7 %all-gather.28.cloned.1.call-start = ((), (), s32[]{:S(2)}) async-start(), calls=%async_computation.13 | async-start | bytes 3686400 | tf_op jit(solution)/shard_map/all_gather | solution.py:210
  15.2 344.2 %all-gather.30.cloned.1.call-start = ((), (), s32[]{:S(2)}) async-start(), calls=%async_computation.14 | async-start | bytes 14745600 | tf_op jit(solution)/shard_map/all_gather | solution.py:211
  16.0 419.8 %all-gather.32.cloned.1.call-start = ((), (), s32[]{:S(2)}) async-start(), calls=%async_computation.15 | async-start | bytes 14745600 | tf_op jit(solution)/shard_map/all_gather | solution.py:212
  16.7 478.6 %all-gather.34.cloned.1.call-start = ((), (), s32[]{:S(2)}) async-start(), calls=%async_computation.16 | async-start | bytes 2949120 | tf_op jit(solution)/shard_map/all_gather | solution.py:213
  17.3 771.3 %reduce-scatter.22.cloned.1.call-start = ((), (), s32[]{:S(2)}) async-start(), calls=%async_computation.22 | async-start | bytes 884736 | tf_op jit(solution)/shard_map/reduce_scatter | solution.py:291
  186.8 478.7 %copy-start.7 = (f32[2,228,768]{2,1,0:T(8,128)}, f32[2,228,768]{2,1,0:T(8,128)S(1)}, u32[]{:S(2)}) copy-start(f32[2,228,768]{2,1,0:T(8,128)S(1)} %get-tuple-element.212) | copy-start | bytes 4202500
  497.9 5.3 collective-permute-start
  502.5 3.6 collective-permute-start.5
  503.2 4.6 collective-permute-start.1
  506.1 4.6 collective-permute-start.6
  507.8 3.0 collective-permute-start.2
  510.8 5.8 collective-permute-start.7
  510.9 4.0 collective-permute-start.3
  514.9 73.8 %collective-permute-start.4 = (bf16[32,1024]{1,0:T(8,128)(2,1)S(1)}, bf16[32,1024]{1,0:T(8,128)(2,1)S(1)}, u32[]{:S(2)}, u32[]{:S(2)}) collective-permute-start(bf16[32,1024]{1,0:T(8,128)(2,1)S(1)} %concatenate.44), channel_id=1, source_target_pairs={{0,16},{1,17},{2,18},{3,19},{4,20},{5,21},{6,22},{7,23},{8,24},{9,... | collective-permute-start | bytes 196616 | tf_op jit(solution)/shard_map/ppermute | solution.py:29
  516.6 71.5 %collective-permute-start.8 = (bf16[16,1024]{1,0:T(8,128)(2,1)S(1)}, bf16[16,1024]{1,0:T(8,128)(2,1)S(1)}, u32[]{:S(2)}, u32[]{:S(2)}) collective-permute-start(bf16[16,1024]{1,0:T(8,128)(2,1)S(1)} %pad_maximum_fusion.3), channel_id=1, source_target_pairs={{0,24},{1,25},{2,26},{3,27},{4,28},{5,29},{6,30},{7,31},{8,0},{9,1... | collective-permute-start | bytes 98312 | tf_op jit(solution)/shard_map/ppermute | solution.py:29
  588.2 71.6 %collective-permute-start.9 = (bf16[32,1024]{1,0:T(8,128)(2,1)S(1)}, bf16[32,1024]{1,0:T(8,128)(2,1)S(1)}, u32[]{:S(2)}, u32[]{:S(2)}) collective-permute-start(bf16[32,1024]{1,0:T(8,128)(2,1)S(1)} %concatenate.49), channel_id=1, source_target_pairs={{0,16},{1,17},{2,18},{3,19},{4,20},{5,21},{6,22},{7,23},{8,24},{9,... | collective-permute-start | bytes 196616 | tf_op jit(solution)/shard_map/ppermute | solution.py:29
  740.0 80.0 %reduce-scatter.14.cloned.1.call-start = ((), (), s32[]{:S(2)}) async-start(), calls=%async_computation.18 | async-start | bytes 2654208 | tf_op jit(solution)/shard_map/reduce_scatter | solution.py:293
  744.6 125.4 %reduce-scatter.20.cloned.1.call-start = ((), (), s32[]{:S(2)}) async-start(), calls=%async_computation.21 | async-start | bytes 3538944 | tf_op jit(solution)/shard_map/reduce_scatter | solution.py:296
  748.9 190.0 %reduce-scatter.12.cloned.1.call-start = ((), (), s32[]{:S(2)}) async-start(), calls=%async_computation.17 | async-start | bytes 7962624 | tf_op jit(solution)/shard_map/reduce_scatter | solution.py:292
  759.0 260.1 %reduce-scatter.18.cloned.1.call-start = ((), (), s32[]{:S(2)}) async-start(), calls=%async_computation.20 | async-start | bytes 10616832 | tf_op jit(solution)/shard_map/reduce_scatter | solution.py:295
  775.8 323.6 %reduce-scatter.16.cloned.1.call-start = ((), (), s32[]{:S(2)}) async-start(), calls=%async_computation.19 | async-start | bytes 10616832 | tf_op jit(solution)/shard_map/reduce_scatter | solution.py:294
  787.4 349.7 %reduce-scatter.24.cloned.1.call-start = ((), (), s32[]{:S(2)}) async-start(), calls=%async_computation.23 | async-start | bytes 442368
  788.5 502.9 %all-reduce.3.cloned.1.call-start = ((), (), s32[]{:S(2)}) async-start(), calls=%async_computation.24 | async-start | bytes 8060928 | tf_op jit(solution)/shard_map/psum | solution.py:300
  1099.4 220.5 %copy-start.126 = (f32[3,96]{1,0:T(4,128)S(1)}, f32[3,96]{1,0:T(4,128)}, u32[]{:S(2)}) copy-start(f32[3,96]{1,0:T(4,128)} %param.49) | copy-start | bytes 3460
  1099.5 221.2 %copy-start.61 = (f32[96,1024]{1,0:T(8,128)S(1)}, f32[96,1024]{1,0:T(8,128)}, u32[]{:S(2)}) copy-start(f32[96,1024]{1,0:T(8,128)} %param.48) | copy-start | bytes 1179652
  1099.5 221.1 %copy-start.82 = (f32[96,1024]{1,0:T(8,128)S(1)}, f32[96,1024]{1,0:T(8,128)}, u32[]{:S(2)}) copy-start(f32[96,1024]{1,0:T(8,128)} %param.55) | copy-start | bytes 1179652
  (148 other events, 2301.5 us)
Sparse Core Ops, SparseCore 0:
  10.5 38.2 all-gather.15
  51.2 24.0 all-gather.17
  77.8 38.9 all-gather.19
  119.1 38.9 all-gather.21
  160.4 25.6 all-gather.23
  187.9 60.4 all-gather.25
  250.3 32.8 all-gather.27
  285.1 74.3 all-gather.29
  361.3 74.3 all-gather.31
  437.5 30.1 all-gather.33
  740.1 34.0 reduce-scatter.21
  777.4 42.4 reduce-scatter.13
  823.7 46.2 reduce-scatter.19
  873.4 65.5 reduce-scatter.11
  942.7 76.4 reduce-scatter.17
  1022.9 76.4 reduce-scatter.15
  1103.2 33.8 reduce-scatter.23
  1140.0 151.4 all-reduce.2
